TPU v7x, 256 devices: a whole 4x4x8 slice. The times are simulated.
256 devices in a mesh: ex: 16 (over y_hi, x, core), co: 16 (over y_lo, z).
Axes of the slice: x: 4, y: 4 (y_hi: 2, y_lo: 2; y = y_hi * 2 + y_lo), z: 8, core: 2. Of those that a mesh axis runs over, the one named last changes fastest.
Arguments:
- train_grads: float32 [16384, 32768], P('ex', 'co')
- queries: float32 [1024, 32768], P('ex', 'co'), may hold values from -6 to 6
- module_ids: int32 [8], replicated, may hold values from 0 to 223
- module_scale: float32 [224], replicated, may hold values from 0.3 to 3
- example_ids: int32 [16384], P('ex'), may hold values from 0 to 16383, as said below
Outputs:
- influence: float32 [1024, 16384], P('co', 'ex')
Inputs may be any that keep to these rules, and one draw needn't show every extreme that they name: `example_ids`: the examples of block s of 1024 rows carry the ids s * 1024 to (s + 1) * 1024 - 1, each once.
All inputs are finite; a program needn't handle non-finite values.
Results may differ from a plain program's by a relative error of at most 0.00008.
Values sent between devices are 32-bit elements; how exact they have to be, the bound alone decides.
No kernel may reach another device: no remote copies, remote signals or barrier semaphores. Data moves between devices by JAX's collectives and lax.ppermute only.
A program may use at most 128 MiB of HBM per device.

v0:
```python
import jax
import jax.numpy as jnp
from jax import lax
from jax.sharding import PartitionSpec as P

PROJ = 4096
CHUNKS = 4
epsilon = 1e-06


def shards(train_grads, queries, module_ids, module_scale, example_ids):
    example_count, coord_count = train_grads.shape
    offset = lax.axis_index("co") * coord_count
    position = offset + lax.iota(jnp.int32, coord_count)
    table_index = lax.iota(jnp.int32, module_scale.shape[0])
    picked = jnp.sum(
        jnp.where(module_ids[:, None] == table_index[None, :], module_scale[None, :], 0.0), axis=1
    )
    window_index = lax.iota(jnp.int32, module_ids.shape[0])
    coord_scale = jnp.sum(
        jnp.where((position // PROJ)[:, None] == window_index[None, :], picked[None, :], 0.0),
        axis=1,
    )
    scaled = queries * coord_scale[None, :]
    squares = jnp.sum(train_grads * train_grads, axis=1)
    norm_total = lax.all_gather(squares, "co").sum(0)
    inverse_norm = lax.rsqrt(norm_total + epsilon)
    rows = queries.shape[0] // CHUNKS
    outs = []
    for k in range(CHUNKS):
        all_q = lax.all_gather(scaled[k * rows : (k + 1) * rows], "ex", axis=0, tiled=True)
        s = lax.dot_general(
            all_q,
            train_grads,
            (((1,), (1,)), ((), ())),
            precision=lax.Precision.HIGH,
            preferred_element_type=jnp.float32,
        )
        outs.append(lax.psum_scatter(s, "co", scatter_dimension=0, tiled=True))
    own = jnp.concatenate(outs, 0)
    normed = own * inverse_norm[None, :]
    local_ids = example_ids - lax.axis_index("ex") * example_count
    return jnp.zeros_like(normed).at[:, local_ids].set(normed)


def solution(mesh):
    return jax.shard_map(
        shards,
        mesh=mesh,
        in_specs=(P("ex", "co"), P("ex", "co"), P(), P(), P("ex")),
        out_specs=P("co", "ex"),
        check_vma=False,
    )
```

profile of v0, /device:TPU:2, one launch (start us, length us, event | category | flops | bytes accessed | tf_op | source)
XLA Modules:
  0.0 527.2 jit_solution(14822634921270370738)
XLA Ops:
  6.5 0.0 all-gather.12.cloned.1.call-start
  6.6 0.9 select_reduce_fusion.1
  7.4 0.1 select_reduce_fusion
  7.5 1.1 broadcast_multiply_fusion
  8.6 0.8 fusion.6
  9.4 0.0 all-gather.12.cloned.1.call-update
  9.4 0.0 all-gather.6.cloned.1.call-start
  9.5 0.7 all-gather.6.cloned.1.call-update
  10.2 0.0 all-gather.8.cloned.1.call-start
  10.2 0.7 all-gather.8.cloned.1.call-update
  10.9 0.0 all-gather.10.cloned.1.call-start
  11.0 0.5 all-gather.10.cloned.1.call-update
  11.5 0.0 reduce-scatter.11.cloned.1.call-start
  11.5 54.8 %all-gather.12.cloned.1.call-done = f32[256,2048]{1,0:T(8,128)} async-done(((f32[16,2048]{1,0:T(8,128)}), f32[256,2048]{1,0:T(8,128)}) %all-gather.12.cloned.1.call-update) | async-done | bytes 2097168 | tf_op jit(solution)/shard_map/all_gather | solution.py:31
  66.3 8.7 %fusion.10 = f32[256,1024]{1,0:T(8,128)} fusion(f32[256,2048]{1,0:T(8,128)} %all-gather.12.cloned.1.call-done, f32[1024,2048]{1,0:T(8,128)} %param.5), kind=kOutput, calls=%fused_computation.26 | convolution fusion | flops 3221225472 | bytes 11534336 | tf_op jit(solution)/shard_map/dot_general | solution.py:32
  75.0 0.0 reduce-scatter.11.cloned.1.call-update
  75.0 0.0 reduce-scatter.5.cloned.1.call-start
  75.1 46.4 %all-gather.6.cloned.1.call-done = f32[256,2048]{1,0:T(8,128)} async-done(((f32[16,2048]{1,0:T(8,128)}), f32[256,2048]{1,0:T(8,128)}) %all-gather.6.cloned.1.call-update) | async-done | bytes 2097168 | tf_op jit(solution)/shard_map/all_gather | solution.py:31
  121.5 8.6 %fusion.7 = f32[256,1024]{1,0:T(8,128)} fusion(f32[256,2048]{1,0:T(8,128)} %all-gather.6.cloned.1.call-done, f32[1024,2048]{1,0:T(8,128)} %param.5), kind=kOutput, calls=%fused_computation.23 | convolution fusion | flops 3221225472 | bytes 11534336 | tf_op jit(solution)/shard_map/dot_general | solution.py:32
  130.1 0.0 reduce-scatter.5.cloned.1.call-update
  130.1 0.0 reduce-scatter.7.cloned.1.call-start
  130.2 46.5 %all-gather.8.cloned.1.call-done = f32[256,2048]{1,0:T(8,128)} async-done(((f32[16,2048]{1,0:T(8,128)}), f32[256,2048]{1,0:T(8,128)}) %all-gather.8.cloned.1.call-update) | async-done | bytes 2097168 | tf_op jit(solution)/shard_map/all_gather | solution.py:31
  176.6 8.6 %fusion.8 = f32[256,1024]{1,0:T(8,128)} fusion(f32[256,2048]{1,0:T(8,128)} %all-gather.8.cloned.1.call-done, f32[1024,2048]{1,0:T(8,128)} %param.5), kind=kOutput, calls=%fused_computation.24 | convolution fusion | flops 3221225472 | bytes 11534336 | tf_op jit(solution)/shard_map/dot_general | solution.py:32
  185.2 0.0 reduce-scatter.7.cloned.1.call-update
  185.3 0.2 reduce-scatter.9.cloned.1.call-start
  185.5 46.1 %all-gather.10.cloned.1.call-done = f32[256,2048]{1,0:T(8,128)} async-done(((f32[16,2048]{1,0:T(8,128)}), f32[256,2048]{1,0:T(8,128)}) %all-gather.10.cloned.1.call-update) | async-done | bytes 2097168 | tf_op jit(solution)/shard_map/all_gather | solution.py:31
  231.6 8.6 %fusion.9 = f32[256,1024]{1,0:T(8,128)} fusion(f32[256,2048]{1,0:T(8,128)} %all-gather.10.cloned.1.call-done, f32[1024,2048]{1,0:T(8,128)} %param.5), kind=kOutput, calls=%fused_computation.25 | convolution fusion | flops 3221225472 | bytes 11534336 | tf_op jit(solution)/shard_map/dot_general | solution.py:32
  240.2 0.0 reduce-scatter.9.cloned.1.call-update
  240.3 0.0 copy-start
  240.3 4.0 multiply_reduce_fusion
  244.3 33.3 %all-gather = f32[16384]{0:T(1024)S(1)} all-gather(f32[1024]{0:T(1024)S(1)} %multiply_reduce_fusion), channel_id=2, replica_groups=mesh['ex'=16,'co'=16] {'co'}, dimensions={0}, use_global_device_ids=true | all-gather | bytes 69632 | tf_op jit(solution)/shard_map/all_gather | solution.py:26
  277.6 0.0 copy-done
  277.7 27.0 %reduce-scatter.11.cloned.1.call-done = f32[16,1024]{1,0:T(8,128)} async-done(((f32[256,1024]{1,0:T(8,128)}), f32[16,1024]{1,0:T(8,128)}) %reduce-scatter.11.cloned.1.call-update) | async-done | bytes 65552 | tf_op jit(solution)/shard_map/reduce_scatter | solution.py:39
  304.6 70.1 %reduce-scatter.5.cloned.1.call-done = f32[16,1024]{1,0:T(8,128)} async-done(((f32[256,1024]{1,0:T(8,128)}), f32[16,1024]{1,0:T(8,128)}) %reduce-scatter.5.cloned.1.call-update) | async-done | bytes 65552 | tf_op jit(solution)/shard_map/reduce_scatter | solution.py:39
  374.8 70.1 %reduce-scatter.7.cloned.1.call-done = f32[16,1024]{1,0:T(8,128)} async-done(((f32[256,1024]{1,0:T(8,128)}), f32[16,1024]{1,0:T(8,128)}) %reduce-scatter.7.cloned.1.call-update) | async-done | bytes 65552 | tf_op jit(solution)/shard_map/reduce_scatter | solution.py:39
  444.8 70.2 %reduce-scatter.9.cloned.1.call-done = f32[16,1024]{1,0:T(8,128)} async-done(((f32[256,1024]{1,0:T(8,128)}), f32[16,1024]{1,0:T(8,128)}) %reduce-scatter.9.cloned.1.call-update) | async-done | bytes 65552 | tf_op jit(solution)/shard_map/reduce_scatter | solution.py:39
  515.1 1.0 fusion
  516.0 0.2 copy.10
  516.2 3.2 scatter_custom_fusion
  519.5 0.9 copy.11
  (5 shorter events, 0.1 us)
Async XLA Ops:
  6.5 59.8 %all-gather.12.cloned.1.call-start = ((), (), s32[]{:S(2)}) async-start(), calls=%async_computation.10 | async-start | bytes 2228224 | tf_op jit(solution)/shard_map/all_gather | solution.py:31
  9.4 112.0 %all-gather.6.cloned.1.call-start = ((), (), s32[]{:S(2)}) async-start(), calls=%async_computation.4 | async-start | bytes 2228224 | tf_op jit(solution)/shard_map/all_gather | solution.py:31
  10.2 166.5 %all-gather.8.cloned.1.call-start = ((), (), s32[]{:S(2)}) async-start(), calls=%async_computation.6 | async-start | bytes 2228224 | tf_op jit(solution)/shard_map/all_gather | solution.py:31
  10.9 220.7 %all-gather.10.cloned.1.call-start = ((), (), s32[]{:S(2)}) async-start(), calls=%async_computation.8 | async-start | bytes 2228224 | tf_op jit(solution)/shard_map/all_gather | solution.py:31
  11.5 293.1 %reduce-scatter.11.cloned.1.call-start = ((), (), s32[]{:S(2)}) async-start(), calls=%async_computation.11 | async-start | bytes 1114112 | tf_op jit(solution)/shard_map/reduce_scatter | solution.py:39
  75.0 299.7 %reduce-scatter.5.cloned.1.call-start = ((), (), s32[]{:S(2)}) async-start(), calls=%async_computation.5 | async-start | bytes 1114112 | tf_op jit(solution)/shard_map/reduce_scatter | solution.py:39
  130.1 314.7 %reduce-scatter.7.cloned.1.call-start = ((), (), s32[]{:S(2)}) async-start(), calls=%async_computation.7 | async-start | bytes 1114112 | tf_op jit(solution)/shard_map/reduce_scatter | solution.py:39
  185.3 329.8 %reduce-scatter.9.cloned.1.call-start = ((), (), s32[]{:S(2)}) async-start(), calls=%async_computation.9 | async-start | bytes 1114112 | tf_op jit(solution)/shard_map/reduce_scatter | solution.py:39
  240.3 37.4 %copy-start = (s32[1024]{0:T(1024)S(1)}, s32[1024]{0:T(1024)}, u32[]{:S(2)}) copy-start(s32[1024]{0:T(1024)} %param.9) | copy-start | bytes 12292
Sparse Core Ops, SparseCore 0:
  10.1 56.1 all-gather.11
  69.1 52.3 all-gather.5
  124.2 52.3 all-gather.7
  179.2 52.3 all-gather.9
  234.0 70.5 reduce-scatter.10
  307.1 67.5 reduce-scatter.4
  377.3 67.5 reduce-scatter.6
  447.5 67.5 reduce-scatter.8
where the time goes:
time: 527 us
  waiting for transfers between devices  433 us (82%)
  matrix products  34.5 us (7%)
  blocking collectives  33.3 us (6%)
  between operations  13.6 us (3%)
  other arithmetic  7.04 us (1%)
    reduce_scatter x4, waiting for transfers between devices, shards(): outs.append(lax.psum_scatter(s, 'co', scatter_dimension=0, tiled=True))  237 us
    all_gather x4, waiting for transfers between devices, shards(): lax.all_gather(scaled[k * rows:(k + 1) * rows], 'ex', axis=0, tiled=True)  194 us
    dot_general x4, matrix products, shards(): lax.dot_general(all_q, train_grads, (((1,), (1,)), ((), ())), precision=l...  34.5 us
    all_gather x1, blocking collectives, shards(): norm_total = lax.all_gather(squares, 'co').sum(0)  33.3 us
  transfers between devices with their start and end apart: 8, of which 8 were waited for; matrix products, arithmetic and copies ran while one was open for 7% of the time, Pallas kernels for 0%

commit v1 on v0

--- a/solution.py
+++ b/solution.py
@@ -28,7 +28,12 @@
     rows = queries.shape[0] // CHUNKS
     outs = []
     for k in range(CHUNKS):
-        all_q = lax.all_gather(scaled[k * rows : (k + 1) * rows], "ex", axis=0, tiled=True)
+        all_q = jnp.concatenate(
+            lax.all_to_all(
+                jnp.stack([scaled[k * rows : (k + 1) * rows]] * lax.axis_size("ex")), "ex", 0, 0
+            ),
+            axis=0,
+        )
         s = lax.dot_general(
             all_q,
             train_grads,

time: 527 us -> 365 us (0.69)
  waiting for transfers between devices: 433 us -> 214 us
  blocking collectives: 33.3 us -> 68.9 us
  starting transfers between devices: 0.46 us -> 19 us
    all_gather x4 -> x0, waiting for transfers between devices: 194 us -> none  [shards(): lax.all_gather(scaled[k * rows:(k + 1) * rows], 'ex', axis=0, tiled=True)]
    reduce_scatter x4, waiting for transfers between devices: 237 us -> 150 us  [shards(): outs.append(lax.psum_scatter(s, 'co', scatter_dimension=0, tiled=True))]
    all_to_all x0 -> x3, waiting for transfers between devices: none -> 64.1 us  [shards(): lax.all_to_all(jnp.stack([scaled[k * rows:(k + 1) * rows]] * lax.axis_siz...]
    all_to_all x0 -> x1, blocking collectives: none -> 33 us  [shards(): lax.all_to_all(jnp.stack([scaled[k * rows:(k + 1) * rows]] * lax.axis_siz...]
    all_to_all x0 -> x3, starting transfers between devices: none -> 18.6 us  [shards(): lax.all_to_all(jnp.stack([scaled[k * rows:(k + 1) * rows]] * lax.axis_siz...]
  transfers between devices with their start and end apart: 8 -> 7, of which waited for: 8 -> 6; matrix products, arithmetic and copies ran while one was open for 7% -> 11% of each run, Pallas kernels for 0% -> 0%
where the time goes in v1:
time: 365 us
  waiting for transfers between devices  214 us (59%)
  blocking collectives  68.9 us (19%)
  matrix products  32.9 us (9%)
  starting transfers between devices  19 us (5%)
  between operations  13.2 us (4%)
  local copies, waits for them, and re-layouts  9.69 us (3%)
  other arithmetic  7.04 us (2%)
    reduce_scatter x4, waiting for transfers between devices, shards(): outs.append(lax.psum_scatter(s, 'co', scatter_dimension=0, tiled=True))  150 us
    all_to_all x3, waiting for transfers between devices, shards(): lax.all_to_all(jnp.stack([scaled[k * rows:(k + 1) * rows]] * lax.axis_siz...  64.1 us
    all_gather x1, blocking collectives, shards(): norm_total = lax.all_gather(squares, 'co').sum(0)  35.9 us
    all_to_all x1, blocking collectives, shards(): lax.all_to_all(jnp.stack([scaled[k * rows:(k + 1) * rows]] * lax.axis_siz...  33 us
    dot_general x4, matrix products, shards(): lax.dot_general(all_q, train_grads, (((1,), (1,)), ((), ())), precision=l...  32.9 us
    all_to_all x3, starting transfers between devices, shards(): lax.all_to_all(jnp.stack([scaled[k * rows:(k + 1) * rows]] * lax.axis_siz...  18.6 us
  transfers between devices with their start and end apart: 7, of which 6 were waited for; matrix products, arithmetic and copies ran while one was open for 11% of the time, Pallas kernels for 0%

profile of v1, /device:TPU:2, one launch (start us, length us, event | category | flops | bytes accessed | tf_op | source)
XLA Modules:
  0.0 364.7 jit_solution(12885031734569632190)
XLA Ops:
  6.5 0.9 select_reduce_fusion.1
  7.4 0.1 select_reduce_fusion
  7.5 1.1 broadcast_multiply_fusion
  8.6 0.2 stack.11
  8.9 33.0 %all_to_all.20 = f32[16,16,2048]{2,1,0:T(8,128)} all-to-all(f32[16,16,2048]{2,1,0:T(8,128)S(1)} %stack.11), channel_id=1, replica_groups=mesh['ex'=16,'co'=16] {'ex'}, dimensions={0} | all-to-all | bytes 4194304 | tf_op jit(solution)/shard_map/all_to_all | solution.py:32
  41.8 1.6 stack.8
  43.4 7.2 %all-to-all-start = ((f32[16,16,2048]{2,1,0:T(8,128)}), f32[16,16,2048]{2,1,0:T(8,128)S(1)}, u32[]{:S(2)}, u32[]{:S(2)}) async-start(f32[16,16,2048]{2,1,0:T(8,128)} %stack.8), calls=%async_computation | async-start | bytes 4194304 | tf_op jit(solution)/shard_map/all_to_all | solution.py:32
  50.7 0.0 reduce-scatter.11.cloned.1.call-start
  50.7 8.6 %fusion.10 = f32[256,1024]{1,0:T(8,128)} fusion(f32[256,2048]{1,0:T(8,128)} %bitcast.16, f32[1024,2048]{1,0:T(8,128)} %param.5), kind=kOutput, calls=%fused_computation.26 | convolution fusion | flops 3221225472 | bytes 11534336 | tf_op jit(solution)/shard_map/dot_general | solution.py:37
  59.3 0.0 reduce-scatter.11.cloned.1.call-update
  59.3 19.9 %all-to-all-done = f32[16,16,2048]{2,1,0:T(8,128)S(1)} async-done(((f32[16,16,2048]{2,1,0:T(8,128)}), f32[16,16,2048]{2,1,0:T(8,128)S(1)}, u32[]{:S(2)}, u32[]{:S(2)}) %all-to-all-start) | async-done | bytes 2097184 | tf_op jit(solution)/shard_map/all_to_all | solution.py:32
  79.2 0.0 copy-start
  79.2 1.7 stack.9
  81.0 0.2 copy-done
  81.2 5.6 %all-to-all-start.1 = ((f32[16,16,2048]{2,1,0:T(8,128)}), f32[16,16,2048]{2,1,0:T(8,128)S(1)}, u32[]{:S(2)}, u32[]{:S(2)}) async-start(f32[16,16,2048]{2,1,0:T(8,128)} %stack.9), calls=%async_computation.2 | async-start | bytes 4194304 | tf_op jit(solution)/shard_map/all_to_all | solution.py:32
  86.8 0.0 reduce-scatter.5.cloned.1.call-start
  86.9 8.7 %fusion.7 = f32[256,1024]{1,0:T(8,128)} fusion(f32[256,2048]{1,0:T(8,128)} %bitcast.15, f32[1024,2048]{1,0:T(8,128)} %param.5), kind=kOutput, calls=%fused_computation.23 | convolution fusion | flops 3221225472 | bytes 11534336 | tf_op jit(solution)/shard_map/dot_general | solution.py:37
  95.5 0.0 reduce-scatter.5.cloned.1.call-update
  95.6 22.2 %all-to-all-done.1 = f32[16,16,2048]{2,1,0:T(8,128)S(1)} async-done(((f32[16,16,2048]{2,1,0:T(8,128)}), f32[16,16,2048]{2,1,0:T(8,128)S(1)}, u32[]{:S(2)}, u32[]{:S(2)}) %all-to-all-start.1) | async-done | bytes 2097184 | tf_op jit(solution)/shard_map/all_to_all | solution.py:32
  117.8 1.5 stack.10
  119.3 5.8 %all-to-all-start.2 = ((f32[16,16,2048]{2,1,0:T(8,128)}), f32[16,16,2048]{2,1,0:T(8,128)}, u32[]{:S(2)}, u32[]{:S(2)}) async-start(f32[16,16,2048]{2,1,0:T(8,128)} %stack.10), calls=%async_computation.4 | async-start | bytes 4194304 | tf_op jit(solution)/shard_map/all_to_all | solution.py:32
  125.1 0.0 reduce-scatter.7.cloned.1.call-start
  125.1 7.0 %fusion.8 = f32[256,1024]{1,0:T(8,128)} fusion(f32[256,2048]{1,0:T(8,128)S(1)} %bitcast.14, f32[1024,2048]{1,0:T(8,128)} %param.5), kind=kOutput, calls=%fused_computation.24 | convolution fusion | flops 3221225472 | bytes 11534336 | tf_op jit(solution)/shard_map/dot_general | solution.py:37
  132.2 0.0 reduce-scatter.7.cloned.1.call-update
  132.2 0.2 reduce-scatter.9.cloned.1.call-start
  132.4 22.0 %all-to-all-done.2 = f32[16,16,2048]{2,1,0:T(8,128)} async-done(((f32[16,16,2048]{2,1,0:T(8,128)}), f32[16,16,2048]{2,1,0:T(8,128)}, u32[]{:S(2)}, u32[]{:S(2)}) %all-to-all-start.2) | async-done | bytes 2097184 | tf_op jit(solution)/shard_map/all_to_all | solution.py:32
  154.4 8.6 %fusion.9 = f32[256,1024]{1,0:T(8,128)} fusion(f32[256,2048]{1,0:T(8,128)} %bitcast.2, f32[1024,2048]{1,0:T(8,128)} %param.5), kind=kOutput, calls=%fused_computation.25 | convolution fusion | flops 3221225472 | bytes 11534336 | tf_op jit(solution)/shard_map/dot_general | solution.py:37
  163.0 0.0 reduce-scatter.9.cloned.1.call-update
  163.0 0.0 copy-start.1
  163.0 4.0 %multiply_reduce_fusion = f32[1024]{0:T(1024)S(1)} fusion(f32[1024,2048]{1,0:T(8,128)} %param.5), kind=kLoop, calls=%fused_computation.1 | loop fusion | flops 4193280 | bytes 8392704 | tf_op jit(solution)/shard_map/reduce_sum | solution.py:25
  167.0 35.9 %all-gather = f32[16384]{0:T(1024)S(1)} all-gather(f32[1024]{0:T(1024)S(1)} %multiply_reduce_fusion), channel_id=2, replica_groups=mesh['ex'=16,'co'=16] {'co'}, dimensions={0}, use_global_device_ids=true | all-gather | bytes 69632 | tf_op jit(solution)/shard_map/all_gather | solution.py:26
  203.0 0.0 copy-done.1
  203.1 0.0 reduce-scatter.11.cloned.1.call-done
  203.1 9.6 %reduce-scatter.5.cloned.1.call-done = f32[16,1024]{1,0:T(8,128)} async-done(((f32[256,1024]{1,0:T(8,128)}), f32[16,1024]{1,0:T(8,128)}) %reduce-scatter.5.cloned.1.call-update) | async-done | bytes 65552 | tf_op jit(solution)/shard_map/reduce_scatter | solution.py:44
  212.7 70.1 %reduce-scatter.7.cloned.1.call-done = f32[16,1024]{1,0:T(8,128)} async-done(((f32[256,1024]{1,0:T(8,128)}), f32[16,1024]{1,0:T(8,128)}) %reduce-scatter.7.cloned.1.call-update) | async-done | bytes 65552 | tf_op jit(solution)/shard_map/reduce_scatter | solution.py:44
  282.8 70.1 %reduce-scatter.9.cloned.1.call-done = f32[16,1024]{1,0:T(8,128)} async-done(((f32[256,1024]{1,0:T(8,128)}), f32[16,1024]{1,0:T(8,128)}) %reduce-scatter.9.cloned.1.call-update) | async-done | bytes 65552 | tf_op jit(solution)/shard_map/reduce_scatter | solution.py:44
  352.9 1.0 fusion
  353.8 0.2 copy.10
  354.0 3.2 scatter_custom_fusion
  357.3 0.9 copy.11
  (6 shorter events, 0.1 us)
Async XLA Ops:
  43.4 35.8 %all-to-all-start = ((f32[16,16,2048]{2,1,0:T(8,128)}), f32[16,16,2048]{2,1,0:T(8,128)S(1)}, u32[]{:S(2)}, u32[]{:S(2)}) async-start(f32[16,16,2048]{2,1,0:T(8,128)} %stack.8), calls=%async_computation | async-start | bytes 4194304 | tf_op jit(solution)/shard_map/all_to_all | solution.py:32
  50.7 152.4 %reduce-scatter.11.cloned.1.call-start = ((), (), s32[]{:S(2)}) async-start(), calls=%async_computation.11 | async-start | bytes 1114112 | tf_op jit(solution)/shard_map/reduce_scatter | solution.py:44
  79.2 2.0 copy-start
  81.2 36.6 %all-to-all-start.1 = ((f32[16,16,2048]{2,1,0:T(8,128)}), f32[16,16,2048]{2,1,0:T(8,128)S(1)}, u32[]{:S(2)}, u32[]{:S(2)}) async-start(f32[16,16,2048]{2,1,0:T(8,128)} %stack.9), calls=%async_computation.2 | async-start | bytes 4194304 | tf_op jit(solution)/shard_map/all_to_all | solution.py:32
  86.8 125.9 %reduce-scatter.5.cloned.1.call-start = ((), (), s32[]{:S(2)}) async-start(), calls=%async_computation.8 | async-start | bytes 1114112 | tf_op jit(solution)/shard_map/reduce_scatter | solution.py:44
  119.3 35.1 %all-to-all-start.2 = ((f32[16,16,2048]{2,1,0:T(8,128)}), f32[16,16,2048]{2,1,0:T(8,128)}, u32[]{:S(2)}, u32[]{:S(2)}) async-start(f32[16,16,2048]{2,1,0:T(8,128)} %stack.10), calls=%async_computation.4 | async-start | bytes 4194304 | tf_op jit(solution)/shard_map/all_to_all | solution.py:32
  125.1 157.7 %reduce-scatter.7.cloned.1.call-start = ((), (), s32[]{:S(2)}) async-start(), calls=%async_computation.9 | async-start | bytes 1114112 | tf_op jit(solution)/shard_map/reduce_scatter | solution.py:44
  132.2 220.7 %reduce-scatter.9.cloned.1.call-start = ((), (), s32[]{:S(2)}) async-start(), calls=%async_computation.10 | async-start | bytes 1114112 | tf_op jit(solution)/shard_map/reduce_scatter | solution.py:44
  163.0 40.0 %copy-start.1 = (s32[1024]{0:T(1024)S(1)}, s32[1024]{0:T(1024)}, u32[]{:S(2)}) copy-start(s32[1024]{0:T(1024)} %param.9) | copy-start | bytes 12292
Sparse Core Ops, SparseCore 0:
  59.5 84.6 reduce-scatter.10
  146.8 65.8 reduce-scatter.4
  215.2 67.5 reduce-scatter.6
  285.3 67.4 reduce-scatter.8
